TPU v7x, 256 devices: a whole 4x4x8 slice. The times are simulated.
256 devices in a mesh: fsdp: 64 (over z, x_hi, y), tp: 4 (over x_lo, core).
Axes of the slice: x: 4 (x_hi: 2, x_lo: 2; x = x_hi * 2 + x_lo), y: 4, z: 8, core: 2. Of those that a mesh axis runs over, the one named last changes fastest.
Arguments:
- tokens: bfloat16 [24576, 8192], P('fsdp', 'tp'), may hold values from -16 to 16
- cotangent: bfloat16 [24576, 1024], P('fsdp', 'tp'), may hold values from -6 to 6
- response_mask: int32 [24576], P('fsdp'), may hold values 0 or 1
- key_weight: bfloat16 [8192, 1024], P('fsdp', 'tp'), may hold values from -0.0625 to 0.0625
- new_hidden: bfloat16 [256, 8, 8192], P('fsdp'), may hold values from -6 to 6
- new_values: bfloat16 [256, 8, 1024], P('fsdp', None, 'tp'), may hold values from -6 to 6
- queries: bfloat16 [256, 8, 8192], P('fsdp', None, 'tp'), may hold values from -16 to 16, as said below
- cache_keys: bfloat16 [256, 2048, 1024], P('fsdp', None, 'tp'), may hold values from -16 to 16, as said below
- cache_values: bfloat16 [256, 2048, 1024], P('fsdp', None, 'tp'), may hold values from -6 to 6
- cache_lengths: int32 [256], P('fsdp'), may hold values from 1 to 2048, as said below
Outputs:
- grad_inputs: bfloat16 [24576, 8192], P('fsdp', 'tp')
- learner_weight: bfloat16 [8192, 1024], P('fsdp', 'tp')
- new_keys: bfloat16 [256, 8, 1024], P('fsdp', None, 'tp')
- context: bfloat16 [256, 8, 8192], P('fsdp', None, 'tp')
Inputs may be any that keep to these rules, and one draw needn't show every extreme that they name: `queries`: queries of the decoded tokens, already rotated. `cache_keys`: cached keys, already rotated. `cache_lengths`: some request has exactly 2048 valid slots.
All inputs are finite; a program needn't handle non-finite values. No bound on the sum of `response_mask` on one device may be relied on, other than what follows from the above.
Results may differ from a plain program's by a relative error of at most 0.0095.
Values may be sent and summed in bfloat16 or wider, within the bound.
No kernel may reach another device: no remote copies, remote signals or barrier semaphores. Data moves between devices by JAX's collectives and lax.ppermute only.
A program may use at most 128 MiB of HBM per device.

v0:
```python
import math
import jax
import jax.numpy as jnp
from jax import lax
from jax.sharding import PartitionSpec as P

D = 8192
HD = 128
ROPE_BASE = 1000000.0


def rope_rotate(keys, positions):
    half = keys.shape[-1] // 2
    freq = ROPE_BASE ** (-jnp.arange(half, dtype=jnp.float32) * (2.0 / keys.shape[-1]))
    angle = positions.astype(jnp.float32)[..., None] * freq
    cosine = jnp.cos(angle)[..., None, :]
    sine = jnp.sin(angle)[..., None, :]
    first = keys[..., :half]
    second = keys[..., half:]
    return jnp.concatenate(
        [first * cosine - second * sine, second * cosine + first * sine], axis=-1
    )


def attend(queries, cache_keys, cache_values, new_keys, new_values, lengths):
    count, steps = (queries.shape[0], queries.shape[1])
    slots = cache_keys.shape[1]
    groups = cache_keys.shape[2] // HD
    share = queries.shape[2] // cache_keys.shape[2]
    inv = 1.0 / math.sqrt(HD)
    query = queries.reshape(count, steps, groups, share, HD)
    old_keys = cache_keys.reshape(count, slots, groups, HD)
    old_values = cache_values.reshape(count, slots, groups, HD)
    fresh_keys = new_keys.reshape(count, steps, groups, HD)
    fresh_values = new_values.reshape(count, steps, groups, HD)
    cache_scores = (
        jnp.einsum("rsjgd,rcjd->rsjgc", query, old_keys, preferred_element_type=jnp.float32) * inv
    )
    fresh_scores = (
        jnp.einsum("rsjgd,rtjd->rsjgt", query, fresh_keys, preferred_element_type=jnp.float32) * inv
    )
    cache_valid = jnp.arange(slots, dtype=jnp.int32)[None, :] < lengths[:, None]
    step_ids = jnp.arange(steps, dtype=jnp.int32)
    fresh_valid = step_ids[None, :] <= step_ids[:, None]
    cache_scores = jnp.where(cache_valid[:, None, None, None, :], cache_scores, -jnp.inf)
    fresh_scores = jnp.where(fresh_valid[None, :, None, None, :], fresh_scores, -jnp.inf)
    top = jnp.maximum(jnp.max(cache_scores, axis=-1), jnp.max(fresh_scores, axis=-1))[..., None]
    cache_exp = jnp.exp(cache_scores - top)
    fresh_exp = jnp.exp(fresh_scores - top)
    total = jnp.sum(cache_exp, axis=-1, keepdims=True) + jnp.sum(fresh_exp, axis=-1, keepdims=True)
    cache_weights = (cache_exp / total).astype(jnp.bfloat16)
    fresh_weights = (fresh_exp / total).astype(jnp.bfloat16)
    mixed = jnp.einsum(
        "rsjgc,rcjd->rsjgd", cache_weights, old_values, preferred_element_type=jnp.float32
    )
    mixed = mixed + jnp.einsum(
        "rsjgt,rtjd->rsjgd", fresh_weights, fresh_values, preferred_element_type=jnp.float32
    )
    return mixed.reshape(count, steps, groups * share * HD).astype(jnp.bfloat16)


def per_device(
    tokens,
    cotangent,
    response_mask,
    key_weight,
    new_hidden,
    new_values,
    queries,
    cache_keys,
    cache_values,
    cache_lengths,
):
    masked = cotangent * response_mask[:, None].astype(jnp.bfloat16)
    rows = key_weight.shape[0]
    scale = 1.0 / math.sqrt(D * tokens.shape[0] * lax.axis_size("fsdp"))
    full_weight = lax.all_gather(key_weight, "fsdp", axis=0, tiled=True)
    whole = lax.all_gather(tokens, "tp", axis=1, tiled=True)
    partial_value = jnp.einsum("tc,tk->ck", whole, masked, preferred_element_type=jnp.float32)
    terms = jnp.einsum("tk,ck->tc", masked, full_weight, preferred_element_type=jnp.float32)
    grad_inputs = lax.psum_scatter(
        terms.astype(jnp.bfloat16), "tp", scatter_dimension=1, tiled=True
    )
    grad = lax.psum(partial_value, "fsdp")
    rollout_weight = (full_weight.astype(jnp.float32) - grad * scale).astype(jnp.bfloat16)
    learner_weight = lax.dynamic_slice_in_dim(
        rollout_weight, lax.axis_index("fsdp") * rows, rows, 0
    )
    requests, steps = (new_hidden.shape[0], new_hidden.shape[1])
    raw = jnp.einsum("rsd,dk->rsk", new_hidden, rollout_weight, preferred_element_type=jnp.float32)
    local_width = raw.shape[2]
    positions = cache_lengths[:, None] + jnp.arange(steps, dtype=jnp.int32)[None, :]
    rotated = rope_rotate(raw.reshape(requests, steps, local_width // HD, HD), positions)
    new_keys = rotated.astype(jnp.bfloat16).reshape(requests, steps, local_width)
    context = attend(queries, cache_keys, cache_values, new_keys, new_values, cache_lengths)
    return (grad_inputs, learner_weight, new_keys, context)


def solution(mesh):
    placed = (
        P("fsdp", "tp"),
        P("fsdp", "tp"),
        P("fsdp"),
        P("fsdp", "tp"),
        P("fsdp", None, None),
        P("fsdp", None, "tp"),
        P("fsdp", None, "tp"),
        P("fsdp", None, "tp"),
        P("fsdp", None, "tp"),
        P("fsdp"),
    )
    return jax.shard_map(
        per_device,
        mesh=mesh,
        in_specs=placed,
        out_specs=(P("fsdp", "tp"), P("fsdp", "tp"), P("fsdp", None, "tp"), P("fsdp", None, "tp")),
        check_vma=False,
    )
```

profile of v0, /device:TPU:1, one launch (start us, length us, event | category | flops | bytes accessed | tf_op | source)
XLA Modules:
  0.0 1011.2 jit_solution(13662762769809048783)
XLA Ops:
  7.2 0.7 all-gather.5.cloned.1.call-update
  7.9 0.0 all-gather.3.cloned.1.call-start
  8.0 1.6 copy.22
  9.6 0.0 all-reduce.2.cloned.1.call-start
  9.6 0.7 convert_element_type.42
  10.3 70.2 %all-gather.5.cloned.1.call-done = bf16[384,8192]{1,0:T(8,128)(2,1)} async-done(((bf16[384,2048]{1,0:T(8,128)(2,1)}), bf16[384,8192]{1,0:T(8,128)(2,1)}) %all-gather.5.cloned.1.call-update) | async-done | bytes 6291472 | tf_op jit(solution)/shard_map/all_gather | solution.py:78
  80.5 8.6 convolution_bitcast_fusion
  89.1 0.0 reduce-scatter.2.cloned.1.call-start
  89.2 120.4 %all-gather.3.cloned.1.call-done = bf16[8192,256]{0,1:T(8,128)(2,1)} async-done(((bf16[128,256]{0,1:T(8,128)(2,1)}), bf16[8192,256]{0,1:T(8,128)(2,1)}) %all-gather.3.cloned.1.call-update) | async-done | bytes 4194320 | tf_op jit(solution)/shard_map/all_gather | solution.py:77
  209.6 6.7 convolution_convert_fusion
  216.3 6.9 reshape.100
  223.2 7.0 reshape.102
  230.3 0.1 add_convert_fusion
  230.4 0.1 multiply_cosine_fusion
  230.5 0.1 iota_compare_fusion
  230.6 5.7 bitcast_reduce_fusion
  236.3 656.1 %all-reduce.2.cloned.1.call-done = f32[8192,256]{0,1:T(8,128)} async-done(((f32[8192,256]{0,1:T(8,128)}), f32[8192,256]{0,1:T(8,128)}) %all-reduce.2.cloned.1.call-update) | async-done | bytes 8388624 | tf_op jit(solution)/shard_map/psum | solution.py:84
  892.5 5.8 subtract_convert_fusion
  898.3 1.3 fusion.17
  899.6 0.1 multiply_subtract_fusion
  899.7 0.7 fusion.33
  900.5 0.1 fusion.20
  900.6 1.4 copy-done.3
  902.0 1.0 fusion.7
  903.0 0.3 copy-done.2
  903.2 1.7 fusion
  905.0 0.3 fusion.16
  905.3 0.7 convert_element_type.53
  906.0 0.8 constant_dynamic-slice_fusion
  906.8 0.7 copy.30
  907.6 0.7 fusion.34
  908.3 96.4 %reduce-scatter.2.cloned.1.call-done = bf16[384,2048]{1,0:T(8,128)(2,1)} async-done(((bf16[384,8192]{1,0:T(8,128)(2,1)}), bf16[384,2048]{1,0:T(8,128)(2,1)}) %reduce-scatter.2.cloned.1.call-update) | async-done | bytes 1572880 | tf_op jit(solution)/shard_map/reduce_scatter | solution.py:81
  (23 shorter events, 0.2 us)
Async XLA Ops:
  7.2 891.1 %copy-start = (bf16[4,8,8192]{2,1,0:T(8,128)(2,1)S(1)}, bf16[4,8,8192]{2,1,0:T(8,128)(2,1)}, u32[]{:S(2)}) copy-start(bf16[4,8,8192]{2,1,0:T(8,128)(2,1)} %param.14) | copy-start | bytes 1572868
  7.2 73.3 %all-gather.5.cloned.1.call-start = ((), (), s32[]{:S(2)}) async-start(), calls=%async_computation.3 | async-start | bytes 7864320 | tf_op jit(solution)/shard_map/all_gather | solution.py:78
  7.9 201.7 %all-gather.3.cloned.1.call-start = ((), (), s32[]{:S(2)}) async-start(), calls=%async_computation.1 | async-start | bytes 4259840 | tf_op jit(solution)/shard_map/all_gather | solution.py:77
  9.6 882.9 %all-reduce.2.cloned.1.call-start = ((), (), s32[]{:S(2)}) async-start(), calls=%async_computation.4 | async-start | bytes 16777216 | tf_op jit(solution)/shard_map/psum | solution.py:84
  89.1 120.5 %copy-start.4 = (bf16[384,256]{1,0:T(8,128)(2,1)S(1)}, bf16[384,256]{1,0:T(8,128)(2,1)}, u32[]{:S(2)}) copy-start(bf16[384,256]{1,0:T(8,128)(2,1)} %param.11) | copy-start | bytes 589828
  89.1 915.5 %reduce-scatter.2.cloned.1.call-start = ((), (), s32[]{:S(2)}) async-start(), calls=%async_computation.2 | async-start | bytes 7864320 | tf_op jit(solution)/shard_map/reduce_scatter | solution.py:81
  223.2 7.1 copy-start.6
  223.2 7.4 copy-start.5
  898.3 2.2 copy-start.1
  898.3 3.7 copy-start.3
  899.6 3.6 copy-start.2
  903.2 1.7 copy-start.7
Sparse Core Ops, SparseCore 0:
  9.8 70.6 all-gather.4
  84.5 125.0 all-gather.2
  212.3 680.1 all-reduce.1
  895.5 109.1 reduce-scatter.1
where the time goes:
time: 1010 us
  waiting for transfers between devices  944 us (93%)
  matrix products  25 us (2%)
  local copies, waits for them, and re-layouts  19.5 us (2%)
  between operations  13.9 us (1%)
    psum x1, waiting for transfers between devices, per_device(): grad = lax.psum(partial_value, 'fsdp')  656 us
    all_gather x1, waiting for transfers between devices, per_device(): full_weight = lax.all_gather(key_weight, 'fsdp', axis=0, tiled=True)  120 us
    reduce_scatter x1, waiting for transfers between devices, per_device(): lax.psum_scatter(terms.astype(jnp.bfloat16), 'tp', scatter_dimension=1, t...  96.4 us
    all_gather x1, waiting for transfers between devices, per_device(): whole = lax.all_gather(tokens, 'tp', axis=1, tiled=True)  70.2 us
  transfers between devices with their start and end apart: 4, of which 4 were waited for; matrix products, arithmetic and copies ran while one was open for 5% of the time, Pallas kernels for 0%

commit v1 on v0

--- a/solution.py
+++ b/solution.py
@@ -75,7 +75,9 @@
     rows = key_weight.shape[0]
     scale = 1.0 / math.sqrt(D * tokens.shape[0] * lax.axis_size("fsdp"))
     full_weight = lax.all_gather(key_weight, "fsdp", axis=0, tiled=True)
-    whole = lax.all_gather(tokens, "tp", axis=1, tiled=True)
+    whole = jnp.concatenate(
+        lax.all_to_all(jnp.stack([tokens] * lax.axis_size("tp")), "tp", 0, 0), axis=1
+    )
     partial_value = jnp.einsum("tc,tk->ck", whole, masked, preferred_element_type=jnp.float32)
     terms = jnp.einsum("tk,ck->tc", masked, full_weight, preferred_element_type=jnp.float32)
     grad_inputs = lax.psum_scatter(

time: 1010 us -> 945 us (0.936)
  waiting for transfers between devices: 944 us -> 864 us
    all_gather x1, waiting for transfers between devices: 120 us -> 39.3 us  [per_device(): full_weight = lax.all_gather(key_weight, 'fsdp', axis=0, tiled=True)]
    all_to_all x0 -> x1, waiting for transfers between devices: none -> 70.4 us  [per_device(): lax.all_to_all(jnp.stack([tokens] * lax.axis_size('tp')), 'tp', 0, 0)]
    all_gather x1 -> x0, waiting for transfers between devices: 70.2 us -> none  [per_device(): whole = lax.all_gather(tokens, 'tp', axis=1, tiled=True)]
  transfers between devices with their start and end apart: 4 -> 4, of which waited for: 4 -> 4; matrix products, arithmetic and copies ran while one was open for 5% -> 6% of each run, Pallas kernels for 0% -> 0%
where the time goes in v1:
time: 945 us; the launch traced here: 944 us
  waiting for transfers between devices  864 us (91%)
  matrix products  25.1 us (3%)
  local copies, waits for them, and re-layouts  24.6 us (3%)
  between operations  13.9 us (1%)
    psum x1, waiting for transfers between devices, per_device(): grad = lax.psum(partial_value, 'fsdp')  658 us
    reduce_scatter x1, waiting for transfers between devices, per_device(): lax.psum_scatter(terms.astype(jnp.bfloat16), 'tp', scatter_dimension=1, t...  96.5 us
    all_to_all x1, waiting for transfers between devices, per_device(): lax.all_to_all(jnp.stack([tokens] * lax.axis_size('tp')), 'tp', 0, 0)  70.4 us
    all_gather x1, waiting for transfers between devices, per_device(): full_weight = lax.all_gather(key_weight, 'fsdp', axis=0, tiled=True)  39.3 us
  transfers between devices with their start and end apart: 4, of which 4 were waited for; matrix products, arithmetic and copies ran while one was open for 6% of the time, Pallas kernels for 0%

profile of v1, /device:TPU:1, one launch (start us, length us, event | category | flops | bytes accessed | tf_op | source)
XLA Modules:
  0.0 944.4 jit_solution(4135705340501004490)
XLA Ops:
  7.2 0.0 all-gather.2.cloned.1.call-start
  7.2 1.6 copy.22
  8.9 1.9 copy.23
  10.8 3.2 stack.2
  13.9 8.5 all-to-all-start
  22.5 70.4 %all-to-all-done = bf16[4,384,2048]{1,2,0:T(8,128)(2,1)} async-done(((bf16[4,384,2048]{1,2,0:T(8,128)(2,1)}), bf16[4,384,2048]{1,2,0:T(8,128)(2,1)}, u32[]{:S(2)}, u32[]{:S(2)}) %all-to-all-start) | async-done | bytes 6291488 | tf_op jit(solution)/shard_map/all_to_all | solution.py:79
  92.9 8.6 convolution_bitcast_fusion
  101.6 0.2 reduce-scatter.2.cloned.1.call-start
  101.8 39.3 %all-gather.2.cloned.1.call-done = bf16[8192,256]{0,1:T(8,128)(2,1)} async-done(((bf16[128,256]{0,1:T(8,128)(2,1)}), bf16[8192,256]{0,1:T(8,128)(2,1)}) %all-gather.2.cloned.1.call-update) | async-done | bytes 4194320 | tf_op jit(solution)/shard_map/all_gather | solution.py:77
  141.1 6.7 convolution_convert_fusion
  147.8 6.9 reshape.110
  154.7 7.0 reshape.112
  161.7 0.1 add_convert_fusion
  161.8 0.1 multiply_cosine_fusion
  161.9 0.1 iota_compare_fusion
  162.0 5.7 bitcast_reduce_fusion
  167.7 657.8 %all-reduce.2.cloned.1.call-done = f32[8192,256]{0,1:T(8,128)} async-done(((f32[8192,256]{0,1:T(8,128)}), f32[8192,256]{0,1:T(8,128)}) %all-reduce.2.cloned.1.call-update) | async-done | bytes 8388624 | tf_op jit(solution)/shard_map/psum | solution.py:86
  825.5 5.8 subtract_convert_fusion
  831.3 1.3 fusion.17
  832.7 0.1 multiply_subtract_fusion
  832.8 0.7 fusion.33
  833.5 0.1 fusion.20
  833.6 1.4 copy-done.3
  835.0 1.0 fusion.7
  836.0 0.3 copy-done.2
  836.3 1.7 fusion
  838.0 0.3 fusion.16
  838.3 0.7 convert_element_type.53
  839.0 0.8 constant_dynamic-slice_fusion
  839.9 0.7 copy.31
  840.6 0.7 fusion.34
  841.3 96.5 %reduce-scatter.2.cloned.1.call-done = bf16[384,2048]{1,0:T(8,128)(2,1)} async-done(((bf16[384,8192]{1,0:T(8,128)(2,1)}), bf16[384,2048]{1,0:T(8,128)(2,1)}) %reduce-scatter.2.cloned.1.call-update) | async-done | bytes 1572880 | tf_op jit(solution)/shard_map/reduce_scatter | solution.py:83
  (26 shorter events, 0.1 us)
Async XLA Ops:
  7.2 824.1 %copy-start = (bf16[4,8,8192]{2,1,0:T(8,128)(2,1)S(1)}, bf16[4,8,8192]{2,1,0:T(8,128)(2,1)}, u32[]{:S(2)}) copy-start(bf16[4,8,8192]{2,1,0:T(8,128)(2,1)} %param.14) | copy-start | bytes 1572868
  7.2 133.9 %all-gather.2.cloned.1.call-start = ((), (), s32[]{:S(2)}) async-start(), calls=%async_computation.2 | async-start | bytes 4259840 | tf_op jit(solution)/shard_map/all_gather | solution.py:77
  13.9 8.5 copy-start.7
  13.9 79.0 %copy-start.4 = (bf16[384,256]{1,0:T(8,128)(2,1)S(1)}, bf16[384,256]{1,0:T(8,128)(2,1)}, u32[]{:S(2)}) copy-start(bf16[384,256]{1,0:T(8,128)(2,1)} %param.11) | copy-start | bytes 589828
  13.9 79.0 %all-to-all-start = ((bf16[4,384,2048]{1,2,0:T(8,128)(2,1)}), bf16[4,384,2048]{1,2,0:T(8,128)(2,1)}, u32[]{:S(2)}, u32[]{:S(2)}) async-start(bf16[4,384,2048]{1,2,0:T(8,128)(2,1)} %stack.2), calls=%async_computation.1 | async-start | bytes 12582912 | tf_op jit(solution)/shard_map/all_to_all | solution.py:79
  22.5 803.1 %all-reduce.2.cloned.1.call-start = ((), (), s32[]{:S(2)}) async-start(), calls=%async_computation.4 | async-start | bytes 16777216 | tf_op jit(solution)/shard_map/psum | solution.py:86
  101.6 836.3 %reduce-scatter.2.cloned.1.call-start = ((), (), s32[]{:S(2)}) async-start(), calls=%async_computation.3 | async-start | bytes 7864320 | tf_op jit(solution)/shard_map/reduce_scatter | solution.py:83
  154.7 7.0 copy-start.6
  154.7 7.3 copy-start.5
  831.3 2.2 copy-start.1
  831.3 3.7 copy-start.3
  832.7 3.6 copy-start.2
  836.3 1.7 copy-start.8
Sparse Core Ops, SparseCore 0:
  12.0 129.0 all-gather.1
  143.7 681.7 all-reduce.1
  828.7 109.1 reduce-scatter.1
